TPU v7x, 32 devices: a whole 2x2x4 slice. The times are simulated.
32 devices in a mesh: dp: 8 (over y, x, core), tensor: 4 (over z).
Axes of the slice: x: 2, y: 2, z: 4, core: 2. Of those that a mesh axis runs over, the one named last changes fastest.
Arguments:
- hidden_in: bfloat16 [4096, 1536], P(('dp', 'tensor')), may hold values from -6 to 6
- positions: int32 [4096], P(('dp', 'tensor')), may hold values from 0 to 511, as said below
- gain_attn: bfloat16 [1536], P(('dp', 'tensor')), may hold values from 0.5 to 1.5
- w_query: bfloat16 [1536, 1536], P(('dp', 'tensor')), may hold values from -0.15625 to 0.15625
- key_matrix: bfloat16 [1536, 768], P(('dp', 'tensor')), may hold values from -0.15625 to 0.15625
- value_matrix: bfloat16 [1536, 768], P(('dp', 'tensor')), may hold values from -0.15625 to 0.15625
- w_output: bfloat16 [1536, 1536], P(('dp', 'tensor')), may hold values from -3.5 to 3.5
- gain_mlp: bfloat16 [1536], P(('dp', 'tensor')), may hold values from 0.5 to 1.5
- w_gate: bfloat16 [1536, 4096], P(None, 'tensor'), may hold values from -0.15625 to 0.15625
- w_up: bfloat16 [1536, 4096], P(None, 'tensor'), may hold values from -0.15625 to 0.15625
- w_down: bfloat16 [4096, 1536], P('tensor'), may hold values from -0.09375 to 0.09375
- cotangent: bfloat16 [4096, 1536], P(('dp', 'tensor')), may hold values from -6 to 6
Outputs:
- layer_out: bfloat16 [4096, 1536], P(('dp', 'tensor'))
- grad_input: float32 [4096, 1536], P(('dp', 'tensor'))
- grad_gain_attn: float32 [1536], P(('dp', 'tensor'))
- grad_w_query: float32 [1536, 1536], P(('dp', 'tensor'))
- grad_w_key: float32 [1536, 768], P(('dp', 'tensor'))
- grad_w_value: float32 [1536, 768], P(('dp', 'tensor'))
- grad_w_output: float32 [1536, 1536], P(('dp', 'tensor'))
- grad_gain_mlp: float32 [1536], P(('dp', 'tensor'))
- grad_w_gate: float32 [1536, 4096], P('dp', 'tensor')
- grad_w_up: float32 [1536, 4096], P('dp', 'tensor')
- grad_w_down: float32 [4096, 1536], P('tensor', 'dp')
Inputs may be any that keep to these rules, and one draw needn't show every extreme that they name: positions is 0 at the first token of every document and at every sequence's first row (multiples of 512), and rises by one from each token to the next within a document; documents are runs of consecutive tokens; the first sequence is a single document of 512 tokens.
All inputs are finite; a program needn't handle non-finite values.
Results may differ from a plain program's by a relative error of at most 0.015.
Values may be sent and summed in bfloat16 or wider, within the bound.
A program may use at most 192 MiB of HBM per device.

v0:
```python
import math
import jax
import jax.numpy as jnp
from jax import lax
from jax.sharding import PartitionSpec as P

QUERY_HEADS = 16
KEY_VALUE_HEADS = 8
HEAD_DIMENSION = 96
EPSILON = 1e-05
ROPE_BASE = 100000.0
MASKED = -1e30


def angle_tables(pos_rows, head_size):
    half_size = head_size // 2
    freq_rates = ROPE_BASE ** (-(jnp.arange(half_size, dtype=jnp.float32) * 2.0) / head_size)
    turned = pos_rows.astype(jnp.float32)[:, None] * freq_rates[None, :]
    return (jnp.cos(turned)[:, None, :], jnp.sin(turned)[:, None, :])


def apply_rotary(tensor_in, cosine_table, sine_table):
    half_size = tensor_in.shape[-1] // 2
    lo_half = tensor_in[..., :half_size]
    hi_half = tensor_in[..., half_size:]
    return jnp.concatenate(
        [
            lo_half * cosine_table - hi_half * sine_table,
            hi_half * cosine_table + lo_half * sine_table,
        ],
        axis=-1,
    )


def shards(
    hidden_in,
    positions,
    gain_attn,
    w_query,
    key_matrix,
    value_matrix,
    w_output,
    gain_mlp,
    w_gate,
    w_up,
    w_down,
    cotangent,
):
    tok_rows = hidden_in.shape[0]
    model_width = hidden_in.shape[1]
    num_heads = QUERY_HEADS
    key_value_count = KEY_VALUE_HEADS
    head_size = HEAD_DIMENSION
    kv_width = key_value_count * head_size
    queries_per_group = num_heads // key_value_count
    seq_len = tok_rows * lax.axis_size("tensor")
    score_scale = 1.0 / math.sqrt(head_size)
    gathered = (
        lax.all_gather(gain_attn, ("dp", "tensor"), axis=0, tiled=True),
        lax.all_gather(w_query, ("dp", "tensor"), axis=0, tiled=True),
        lax.all_gather(key_matrix, ("dp", "tensor"), axis=0, tiled=True),
        lax.all_gather(value_matrix, ("dp", "tensor"), axis=0, tiled=True),
        lax.all_gather(w_output, ("dp", "tensor"), axis=0, tiled=True),
        lax.all_gather(gain_mlp, ("dp", "tensor"), axis=0, tiled=True),
    )
    gain_one, query_full, key_full, value_full, output_full, gain_two = gathered
    gain_one_f = gain_one.astype(jnp.float32)
    gain_two_f = gain_two.astype(jnp.float32)
    x_float = hidden_in.astype(jnp.float32)
    inv_one = lax.rsqrt(jnp.mean(x_float * x_float, axis=-1, keepdims=True) + EPSILON)
    normed_one = (x_float * inv_one * gain_one_f).astype(jnp.bfloat16)
    queries = jnp.dot(normed_one, query_full, preferred_element_type=jnp.float32)
    key_projected = jnp.dot(normed_one, key_full, preferred_element_type=jnp.float32)
    value_proj = jnp.dot(normed_one, value_full, preferred_element_type=jnp.float32)
    cosine_table, sine_table = angle_tables(positions, head_size)
    rotated_query_rows = apply_rotary(
        queries.reshape(tok_rows, num_heads, head_size), cosine_table, sine_table
    ).astype(jnp.bfloat16)
    rotated_key_rows = (
        apply_rotary(
            key_projected.reshape(tok_rows, key_value_count, head_size), cosine_table, sine_table
        )
        .astype(jnp.bfloat16)
        .reshape(tok_rows, kv_width)
    )
    value_rows_lowered = value_proj.astype(jnp.bfloat16)
    keys_all, values_all = (
        lax.all_gather(rotated_key_rows, "tensor", axis=0, tiled=True),
        lax.all_gather(value_rows_lowered, "tensor", axis=0, tiled=True),
    )
    offset = lax.axis_index("tensor") * tok_rows
    query_index = offset + jnp.arange(tok_rows, dtype=jnp.int32)
    key_index = jnp.arange(seq_len, dtype=jnp.int32)
    visible = (key_index[None, :] <= query_index[:, None]) & (
        key_index[None, :] >= (query_index - positions)[:, None]
    )
    visible = jnp.tile(visible, (queries_per_group, 1))

    def split_queries(tensor_in):
        return (
            tensor_in.reshape(tok_rows, key_value_count, queries_per_group, head_size)
            .transpose(1, 2, 0, 3)
            .reshape(key_value_count, queries_per_group * tok_rows, head_size)
        )

    def split_keys(tensor_in):
        return tensor_in.reshape(seq_len, key_value_count, head_size).transpose(1, 0, 2)

    def merge_heads(tensor_in):
        return (
            tensor_in.reshape(key_value_count, queries_per_group, tok_rows, head_size)
            .transpose(2, 0, 1, 3)
            .reshape(tok_rows, model_width)
        )

    query_heads = split_queries(rotated_query_rows)
    k_heads = split_keys(keys_all)
    value_heads = split_keys(values_all)

    def attend(head_items):
        q_block, k_block, v_block = head_items
        scores = (
            jnp.einsum("qd,kd->qk", q_block, k_block, preferred_element_type=jnp.float32)
            * score_scale
        )
        scores = jnp.where(visible, scores, MASKED)
        peak = jnp.max(scores, axis=-1, keepdims=True)
        exp_vals = jnp.exp(scores - peak)
        total = jnp.sum(exp_vals, axis=-1, keepdims=True)
        probs = exp_vals / total
        out_block = jnp.einsum(
            "qk,kd->qd", probs.astype(jnp.bfloat16), v_block, preferred_element_type=jnp.float32
        )
        return (out_block, peak[:, 0] + jnp.log(total[:, 0]))

    attended_rows, log_total = lax.map(attend, (query_heads, k_heads, value_heads))
    attended_low = merge_heads(attended_rows).astype(jnp.bfloat16)
    resid_sum = x_float + jnp.dot(attended_low, output_full, preferred_element_type=jnp.float32)
    inv_two = lax.rsqrt(jnp.mean(resid_sum * resid_sum, axis=-1, keepdims=True) + EPSILON)
    normed_two = (resid_sum * inv_two * gain_two_f).astype(jnp.bfloat16)
    rows_all = lax.all_gather(normed_two, "tensor", axis=0, tiled=True)
    gate_val = jnp.dot(rows_all, w_gate, preferred_element_type=jnp.float32)
    up_val = jnp.dot(rows_all, w_up, preferred_element_type=jnp.float32)
    sig_gate = jax.nn.sigmoid(gate_val)
    silu_gate = gate_val * sig_gate
    act_low = (silu_gate * up_val).astype(jnp.bfloat16)
    mlp_sum = lax.psum_scatter(
        jnp.dot(act_low, w_down, preferred_element_type=jnp.float32).astype(jnp.bfloat16),
        "tensor",
        scatter_dimension=0,
        tiled=True,
    ).astype(jnp.float32)
    layer_out = (resid_sum + mlp_sum).astype(jnp.bfloat16)
    grad_float = cotangent.astype(jnp.float32)
    grad_all = lax.all_gather(cotangent, "tensor", axis=0, tiled=True)
    grad_down = jnp.einsum("sf,sd->fd", act_low, grad_all, preferred_element_type=jnp.float32)
    g_act = jnp.einsum("sd,fd->sf", grad_all, w_down, preferred_element_type=jnp.float32)
    g_gate = (g_act * up_val * sig_gate * (1.0 + gate_val * (1.0 - sig_gate))).astype(jnp.bfloat16)
    g_up = (g_act * silu_gate).astype(jnp.bfloat16)
    grad_gate = jnp.einsum("sd,sf->df", rows_all, g_gate, preferred_element_type=jnp.float32)
    grad_up = jnp.einsum("sd,sf->df", rows_all, g_up, preferred_element_type=jnp.float32)
    g_norm_two = lax.psum_scatter(
        (
            jnp.einsum("sf,df->sd", g_gate, w_gate, preferred_element_type=jnp.float32)
            + jnp.einsum("sf,df->sd", g_up, w_up, preferred_element_type=jnp.float32)
        ).astype(jnp.bfloat16),
        "tensor",
        scatter_dimension=0,
        tiled=True,
    ).astype(jnp.float32)
    scaled_two = gain_two_f * g_norm_two
    grad_gain_two = jnp.sum(g_norm_two * resid_sum * inv_two, axis=0)
    g_resid = (
        grad_float
        + inv_two * scaled_two
        - resid_sum * inv_two**3 * jnp.mean(scaled_two * resid_sum, axis=-1, keepdims=True)
    )
    g_resid_low = g_resid.astype(jnp.bfloat16)
    grad_output = jnp.einsum(
        "tc,td->cd", attended_low, g_resid_low, preferred_element_type=jnp.float32
    )
    g_att = jnp.einsum(
        "td,cd->tc", g_resid_low, output_full, preferred_element_type=jnp.float32
    ).astype(jnp.bfloat16)
    g_heads = split_queries(g_att)

    def attend_back(head_items):
        q_block, k_block, v_block, log_block, g_block = head_items
        scores = (
            jnp.einsum("qd,kd->qk", q_block, k_block, preferred_element_type=jnp.float32)
            * score_scale
        )
        scores = jnp.where(visible, scores, MASKED)
        probs = jnp.exp(scores - log_block[:, None])
        g_probs = jnp.einsum("qd,kd->qk", g_block, v_block, preferred_element_type=jnp.float32)
        g_scores = (probs * (g_probs - jnp.sum(probs * g_probs, axis=-1, keepdims=True))).astype(
            jnp.bfloat16
        )
        g_rq = (
            jnp.einsum("qk,kd->qd", g_scores, k_block, preferred_element_type=jnp.float32)
            * score_scale
        )
        g_rk = (
            jnp.einsum("qk,qd->kd", g_scores, q_block, preferred_element_type=jnp.float32)
            * score_scale
        )
        g_val = jnp.einsum(
            "qk,qd->kd", probs.astype(jnp.bfloat16), g_block, preferred_element_type=jnp.float32
        )
        return (g_rq, g_rk, g_val)

    g_rq, g_rk, g_val = lax.map(
        attend_back, (query_heads, k_heads, value_heads, log_total, g_heads)
    )
    g_rk_flat = g_rk.transpose(1, 0, 2).reshape(seq_len, kv_width)
    g_val_flat = g_val.transpose(1, 0, 2).reshape(seq_len, kv_width)
    key_part, value_part = (
        lax.psum_scatter(
            g_rk_flat.astype(jnp.bfloat16), "tensor", scatter_dimension=0, tiled=True
        ).astype(jnp.float32),
        lax.psum_scatter(
            g_val_flat.astype(jnp.bfloat16), "tensor", scatter_dimension=0, tiled=True
        ).astype(jnp.float32),
    )
    g_queries = (
        apply_rotary(
            merge_heads(g_rq).reshape(tok_rows, num_heads, head_size), cosine_table, -sine_table
        )
        .reshape(tok_rows, model_width)
        .astype(jnp.bfloat16)
    )
    g_keys = (
        apply_rotary(
            key_part.reshape(tok_rows, key_value_count, head_size), cosine_table, -sine_table
        )
        .reshape(tok_rows, kv_width)
        .astype(jnp.bfloat16)
    )
    g_values = value_part.astype(jnp.bfloat16)
    grad_query = jnp.einsum("tc,td->cd", normed_one, g_queries, preferred_element_type=jnp.float32)
    grad_key = jnp.einsum("tc,td->cd", normed_one, g_keys, preferred_element_type=jnp.float32)
    grad_value = jnp.einsum("tc,td->cd", normed_one, g_values, preferred_element_type=jnp.float32)
    g_norm_one = (
        jnp.einsum("td,cd->tc", g_queries, query_full, preferred_element_type=jnp.float32)
        + jnp.einsum("td,cd->tc", g_keys, key_full, preferred_element_type=jnp.float32)
        + jnp.einsum("td,cd->tc", g_values, value_full, preferred_element_type=jnp.float32)
    )
    scaled_one = gain_one_f * g_norm_one
    grad_gain_one = jnp.sum(g_norm_one * x_float * inv_one, axis=0)
    grad_input = (
        g_resid
        + inv_one * scaled_one
        - x_float * inv_one**3 * jnp.mean(scaled_one * x_float, axis=-1, keepdims=True)
    )
    query_part, keyw_part, valuew_part, out_part, gain_one_part, gain_two_part = (
        lax.psum_scatter(grad_query, ("dp", "tensor"), scatter_dimension=0, tiled=True),
        lax.psum_scatter(grad_key, ("dp", "tensor"), scatter_dimension=0, tiled=True),
        lax.psum_scatter(grad_value, ("dp", "tensor"), scatter_dimension=0, tiled=True),
        lax.psum_scatter(grad_output, ("dp", "tensor"), scatter_dimension=0, tiled=True),
        lax.psum_scatter(grad_gain_one, ("dp", "tensor"), scatter_dimension=0, tiled=True),
        lax.psum_scatter(grad_gain_two, ("dp", "tensor"), scatter_dimension=0, tiled=True),
    )
    gate_sum, up_sum, down_sum = (
        lax.psum_scatter(grad_gate, "dp", scatter_dimension=0, tiled=True),
        lax.psum_scatter(grad_up, "dp", scatter_dimension=0, tiled=True),
        lax.psum_scatter(grad_down, "dp", scatter_dimension=1, tiled=True),
    )
    return (
        layer_out,
        grad_input,
        gain_one_part,
        query_part,
        keyw_part,
        valuew_part,
        out_part,
        gain_two_part,
        gate_sum,
        up_sum,
        down_sum,
    )


def solution(mesh):
    placed = (
        P(("dp", "tensor"), None),
        P(("dp", "tensor")),
        P(("dp", "tensor")),
        P(("dp", "tensor"), None),
        P(("dp", "tensor"), None),
        P(("dp", "tensor"), None),
        P(("dp", "tensor"), None),
        P(("dp", "tensor")),
        P(None, "tensor"),
        P(None, "tensor"),
        P("tensor", None),
        P(("dp", "tensor"), None),
    )
    return jax.shard_map(
        shards,
        mesh=mesh,
        in_specs=placed,
        out_specs=(
            P(("dp", "tensor"), None),
            P(("dp", "tensor"), None),
            P(("dp", "tensor")),
            P(("dp", "tensor"), None),
            P(("dp", "tensor"), None),
            P(("dp", "tensor"), None),
            P(("dp", "tensor"), None),
            P(("dp", "tensor")),
            P("dp", "tensor"),
            P("dp", "tensor"),
            P("tensor", "dp"),
        ),
        check_vma=False,
    )
```

profile of v0, /device:TPU:0, one launch (start us, length us, event | category | flops | bytes accessed | tf_op | source)
XLA Modules:
  0.0 1255.0 jit_solution(6569822728411166291)
XLA Ops:
  12.6 42.1 %all-reduce.5 = (bf16[1536]{0:T(1024)(128)(2,1)S(1)}, bf16[1536]{0:T(1024)(128)(2,1)S(1)}) all-reduce(bf16[1536]{0:T(1024)(128)(2,1)S(1)} %dynamic-update-slice, bf16[1536]{0:T(1024)(128)(2,1)S(1)} %dynamic-update-slice.1), channel_id=1, replica_groups=mesh['dp'=8,'tensor'=4] {'dp','tensor'}, use_global_device_ids=true, to_apply=%add | all-reduce | flops 3072 | bytes 12288
  58.7 11.9 all-gather.9.cloned.1.call-done
  73.7 19.5 %all_gather.33 = bf16[512,768]{0,1:T(8,128)(2,1)} all-gather(bf16[128,768]{0,1:T(8,128)(2,1)S(1)} %bitcast.215), channel_id=1, replica_groups=mesh['dp'=8,'tensor'=4] {'tensor'}, dimensions={0}, use_global_device_ids=true | all-gather | bytes 983040 | tf_op jit(solution)/shard_map/all_gather | solution.py:88
  95.4 35.9 %all-gather.11.cloned.1.call-done = bf16[1536,768]{1,0:T(8,128)(2,1)} async-done(((bf16[48,768]{1,0:T(8,128)(2,1)}), bf16[1536,768]{1,0:T(8,128)(2,1)}) %all-gather.11.cloned.1.call-update) | async-done | bytes 2359312 | tf_op jit(solution)/shard_map/all_gather | solution.py:62
  133.5 21.3 %all_gather.35 = bf16[512,768]{1,0:T(8,128)(2,1)} all-gather(bf16[128,768]{1,0:T(8,128)(2,1)S(1)} %convolution_convert_fusion.2), channel_id=1, replica_groups=mesh['dp'=8,'tensor'=4] {'tensor'}, dimensions={0}, use_global_device_ids=true | all-gather | bytes 983040 | tf_op jit(solution)/shard_map/all_gather | solution.py:89
  159.3 38.5 %all-gather.7.cloned.1.call-done = bf16[1536,1536]{1,0:T(8,128)(2,1)} async-done(((bf16[48,1536]{1,0:T(8,128)(2,1)}), bf16[1536,1536]{1,0:T(8,128)(2,1)}) %all-gather.7.cloned.1.call-update) | async-done | bytes 4718608 | tf_op jit(solution)/shard_map/all_gather | solution.py:60
  205.0 48.8 %while.30 = (s32[]{:T(128)}, bf16[8,256,96]{1,2,0:T(8,128)(2,1)}, f32[8,256]{1,0:T(8,128)}, bf16[8,256,96]{2,1,0:T(8,128)(2,1)}, bf16[8,512,96]{2,1,0:T(8,128)(2...) while((s32[]{:T(128)}, bf16[8,256,96]{1,2,0:T(8,128)(2,1)}, ...), condition=%wide.region_4.5_spmd.clone.clone, body=%wide.region_1.4_spmd.clone.sunk.clone | while | flops 51379968 | bytes 2338905 | solution.py:136
  268.5 34.7 %all-gather.15.cloned.1.call-done = bf16[512,1536]{1,0:T(8,128)(2,1)} async-done(((bf16[128,1536]{1,0:T(8,128)(2,1)}), bf16[512,1536]{1,0:T(8,128)(2,1)}) %all-gather.15.cloned.1.call-update) | async-done | bytes 1572880 | tf_op jit(solution)/shard_map/all_gather | solution.py:141
  312.0 28.6 %all-gather.17.cloned.1.call-done = bf16[512,1536]{1,0:T(8,128)(2,1)} async-done(((bf16[128,1536]{1,0:T(8,128)(2,1)}), bf16[512,1536]{1,0:T(8,128)(2,1)}) %all-gather.17.cloned.1.call-update) | async-done | bytes 1572880 | tf_op jit(solution)/shard_map/all_gather | solution.py:155
  340.6 6.3 multiply_convert_fusion.1
  357.0 30.1 %reduce-scatter.18.cloned.1.call-done = bf16[128,1536]{1,0:T(8,128)(2,1)} async-done(((bf16[512,1536]{1,0:T(8,128)(2,1)}), bf16[128,1536]{1,0:T(8,128)(2,1)}) %reduce-scatter.18.cloned.1.call-update) | async-done | bytes 393232 | tf_op jit(solution)/shard_map/reduce_scatter | solution.py:162
  389.1 34.5 %reduce-scatter.16.cloned.1.call-done = bf16[128,1536]{1,0:T(8,128)(2,1)} async-done(((bf16[512,1536]{1,0:T(8,128)(2,1)}), bf16[128,1536]{1,0:T(8,128)(2,1)}) %reduce-scatter.16.cloned.1.call-update) | async-done | bytes 393232 | tf_op jit(solution)/shard_map/reduce_scatter | solution.py:147
  430.7 61.5 %while.31 = (s32[]{:T(128)}, f32[8,256,96]{1,2,0:T(8,128)}, bf16[8,512,96]{1,2,0:T(8,128)(2,1)}, bf16[8,512,96]{1,2,0:T(8,128)(2,1)}, bf16[8,256,96]{2,1,0:T(8,1...) while((s32[]{:T(128)}, f32[8,256,96]{1,2,0:T(8,128)}, ...), condition=%wide.region_11.12_spmd.clone.clone, body=%wide.region_9.11_spmd.clone.sunk.clone | while | flops 127082240 | bytes 5417073 | solution.py:212
  496.1 5.9 fusion.85
  503.3 5.9 fusion.86
  510.4 6.0 fusion.87
  521.2 20.4 %reduce-scatter.36.cloned.1.call-done = bf16[128,768]{1,0:T(8,128)(2,1)} async-done(((bf16[512,768]{1,0:T(8,128)(2,1)}), bf16[128,768]{1,0:T(8,128)(2,1)}) %reduce-scatter.36.cloned.1.call-update) | async-done | bytes 196624
  567.7 40.3 %all-reduce.4 = (f32[1536]{0:T(1024)}, f32[1536]{0:T(1024)}) all-reduce(f32[1536]{0:T(1024)} %get-tuple-element.201, f32[1536]{0:T(1024)} %get-tuple-element.199), channel_id=6, replica_groups=mesh['dp'=8,'tensor'=4] {'dp','tensor'}, use_global_device_ids=true, to_apply=%region_16.17.clone | all-reduce | flops 3072 | bytes 24576
  613.1 60.7 %reduce-scatter.30.cloned.1.call-done = f32[192,1024]{1,0:T(8,128)} async-done(((f32[1536,1024]{1,0:T(8,128)}), f32[192,1024]{1,0:T(8,128)}) %reduce-scatter.30.cloned.1.call-update) | async-done | bytes 786448 | tf_op jit(solution)/shard_map/reduce_scatter | solution.py:265
  673.7 65.7 %reduce-scatter.32.cloned.1.call-done = f32[1024,192]{0,1:T(8,128)} async-done(((f32[1024,1536]{0,1:T(8,128)}), f32[1024,192]{0,1:T(8,128)}) %reduce-scatter.32.cloned.1.call-update) | async-done | bytes 786448 | tf_op jit(solution)/shard_map/reduce_scatter | solution.py:266
  739.5 113.5 %reduce-scatter.22.cloned.1.call-done = f32[48,768]{1,0:T(8,128)} async-done(((f32[1536,768]{1,0:T(8,128)}), f32[48,768]{1,0:T(8,128)}) %reduce-scatter.22.cloned.1.call-update) | async-done | bytes 147472 | tf_op jit(solution)/shard_map/reduce_scatter | solution.py:257
  853.0 112.5 %reduce-scatter.24.cloned.1.call-done = f32[48,768]{1,0:T(8,128)} async-done(((f32[1536,768]{1,0:T(8,128)}), f32[48,768]{1,0:T(8,128)}) %reduce-scatter.24.cloned.1.call-update) | async-done | bytes 147472 | tf_op jit(solution)/shard_map/reduce_scatter | solution.py:258
  965.5 141.5 %reduce-scatter.20.cloned.1.call-done = f32[48,1536]{1,0:T(8,128)} async-done(((f32[1536,1536]{1,0:T(8,128)}), f32[48,1536]{1,0:T(8,128)}) %reduce-scatter.20.cloned.1.call-update) | async-done | bytes 294928 | tf_op jit(solution)/shard_map/reduce_scatter | solution.py:256
  1107.0 141.5 %reduce-scatter.26.cloned.1.call-done = f32[48,1536]{1,0:T(8,128)} async-done(((f32[1536,1536]{1,0:T(8,128)}), f32[48,1536]{1,0:T(8,128)}) %reduce-scatter.26.cloned.1.call-update) | async-done | bytes 294928 | tf_op jit(solution)/shard_map/reduce_scatter | solution.py:259
  (282 shorter events, 223.2 us)
Async XLA Ops:
  7.2 333.4 %copy-start = (bf16[1024,1536]{1,0:T(8,128)(2,1)S(1)}, bf16[1024,1536]{1,0:T(8,128)(2,1)}, u32[]{:S(2)}) copy-start(bf16[1024,1536]{1,0:T(8,128)(2,1)} %param.26) | copy-start | bytes 9437188
  7.2 63.4 %all-gather.9.cloned.1.call-start = ((), (), s32[]{:S(2)}) async-start(), calls=%async_computation.12 | async-start | bytes 2433024 | tf_op jit(solution)/shard_map/all_gather | solution.py:61
  7.9 123.4 %all-gather.11.cloned.1.call-start = ((), (), s32[]{:S(2)}) async-start(), calls=%async_computation.13 | async-start | bytes 2433024 | tf_op jit(solution)/shard_map/all_gather | solution.py:62
  8.7 189.1 %all-gather.7.cloned.1.call-start = ((), (), s32[]{:S(2)}) async-start(), calls=%async_computation.11 | async-start | bytes 4866048 | tf_op jit(solution)/shard_map/all_gather | solution.py:60
  9.4 253.0 %all-gather.13.cloned.1.call-start = ((), (), s32[]{:S(2)}) async-start(), calls=%async_computation.14 | async-start | bytes 4866048 | tf_op jit(solution)/shard_map/all_gather | solution.py:63
  10.0 293.2 %all-gather.15.cloned.1.call-start = ((), (), s32[]{:S(2)}) async-start(), calls=%async_computation.15 | async-start | bytes 1966080 | tf_op jit(solution)/shard_map/all_gather | solution.py:141
  267.7 72.8 %all-gather.17.cloned.1.call-start = ((), (), s32[]{:S(2)}) async-start(), calls=%async_computation.17 | async-start | bytes 1966080 | tf_op jit(solution)/shard_map/all_gather | solution.py:155
  268.3 118.7 %reduce-scatter.18.cloned.1.call-start = ((), (), s32[]{:S(2)}) async-start(), calls=%async_computation.18 | async-start | bytes 1966080 | tf_op jit(solution)/shard_map/reduce_scatter | solution.py:162
  352.6 71.1 %reduce-scatter.16.cloned.1.call-start = ((), (), s32[]{:S(2)}) async-start(), calls=%async_computation.16 | async-start | bytes 1966080 | tf_op jit(solution)/shard_map/reduce_scatter | solution.py:147
  356.8 66.8 %copy-start.4 = (f32[128,1536]{1,0:T(8,128)S(1)}, f32[128,1536]{1,0:T(8,128)}, u32[]{:S(2)}) copy-start(f32[128,1536]{1,0:T(8,128)} %copy-done.3) | copy-start | bytes 2359300
  356.8 66.8 %copy-start.10 = (bf16[128,1536]{1,0:T(8,128)(2,1)S(1)}, bf16[128,1536]{1,0:T(8,128)(2,1)}, u32[]{:S(2)}) copy-start(bf16[128,1536]{1,0:T(8,128)(2,1)} %param.27) | copy-start | bytes 1179652
  356.8 66.8 %copy-start.23 = (f32[128]{0:T(128)S(1)}, f32[128]{0:T(128)}, u32[]{:S(2)}) copy-start(f32[128]{0:T(128)} %copy-done.22) | copy-start | bytes 1540
  356.9 66.8 %copy-start.24 = (f32[128]{0:T(128)S(1)}, f32[128]{0:T(128)}, u32[]{:S(2)}) copy-start(f32[128]{0:T(128)} %get-tuple-element.263) | copy-start | bytes 1540
  356.9 159.9 %reduce-scatter.34.cloned.1.call-start = ((), (), s32[]{:S(2)}) async-start(), calls=%async_computation.26 | async-start | bytes 983040
  425.8 126.8 %copy-start.5 = (f32[128,1536]{1,0:T(8,128)}, f32[128,1536]{1,0:T(8,128)S(1)}, u32[]{:S(2)}) copy-start(f32[128,1536]{1,0:T(8,128)S(1)} %get-tuple-element.252) | copy-start | bytes 2359300
  494.6 47.0 %reduce-scatter.36.cloned.1.call-start = ((), (), s32[]{:S(2)}) async-start(), calls=%async_computation.27 | async-start | bytes 983040
  495.9 117.2 %reduce-scatter.28.cloned.1.call-start = ((), (), s32[]{:S(2)}) async-start(), calls=%async_computation.23 | async-start | bytes 7077888 | tf_op jit(solution)/shard_map/reduce_scatter | solution.py:264
  502.1 171.7 %reduce-scatter.30.cloned.1.call-start = ((), (), s32[]{:S(2)}) async-start(), calls=%async_computation.24 | async-start | bytes 7077888 | tf_op jit(solution)/shard_map/reduce_scatter | solution.py:265
  509.2 230.3 %reduce-scatter.32.cloned.1.call-start = ((), (), s32[]{:S(2)}) async-start(), calls=%async_computation.25 | async-start | bytes 7077888 | tf_op jit(solution)/shard_map/reduce_scatter | solution.py:266
  516.4 336.5 %reduce-scatter.22.cloned.1.call-start = ((), (), s32[]{:S(2)}) async-start(), calls=%async_computation.20 | async-start | bytes 4866048 | tf_op jit(solution)/shard_map/reduce_scatter | solution.py:257
  521.1 444.3 %reduce-scatter.24.cloned.1.call-start = ((), (), s32[]{:S(2)}) async-start(), calls=%async_computation.21 | async-start | bytes 4866048 | tf_op jit(solution)/shard_map/reduce_scatter | solution.py:258
  545.6 561.4 %reduce-scatter.20.cloned.1.call-start = ((), (), s32[]{:S(2)}) async-start(), calls=%async_computation.19 | async-start | bytes 9732096 | tf_op jit(solution)/shard_map/reduce_scatter | solution.py:256
  552.3 696.1 %reduce-scatter.26.cloned.1.call-start = ((), (), s32[]{:S(2)}) async-start(), calls=%async_computation.22 | async-start | bytes 9732096 | tf_op jit(solution)/shard_map/reduce_scatter | solution.py:259
  565.3 683.2 %copy-start.1 = (bf16[1024,1536]{1,0:T(8,128)(2,1)S(1)}, bf16[1024,1536]{1,0:T(8,128)(2,1)}, u32[]{:S(2)}) copy-start(bf16[1024,1536]{1,0:T(8,128)(2,1)} %param.26) | copy-start | bytes 9437188
  (27 other events, 140.1 us)
Sparse Core Ops, SparseCore 0:
  10.8 59.7 all-gather.8
  73.4 57.8 all-gather.10
  134.1 63.6 all-gather.6
  200.4 61.8 all-gather.12
  267.8 35.3 all-gather.14
  304.6 35.8 all-gather.16
  352.7 34.3 reduce-scatter.17
  389.3 34.2 reduce-scatter.15
  494.7 21.9 reduce-scatter.33
  518.9 22.6 reduce-scatter.35
  545.6 62.3 reduce-scatter.27
  611.8 61.9 reduce-scatter.29
  677.7 61.7 reduce-scatter.31
  745.4 107.5 reduce-scatter.21
  858.9 106.5 reduce-scatter.23
  971.8 135.1 reduce-scatter.19
  1113.3 135.1 reduce-scatter.25
where the time goes:
time: 1260 us; the launch traced here: 1250 us
  waiting for transfers between devices  878 us (70%)
  matrix products  164 us (13%)
  blocking collectives  123 us (10%)
  local copies, waits for them, and re-layouts  51.5 us (4%)
  other arithmetic  21.7 us (2%)
  between operations  14.4 us (1%)
    reduce_scatter x1, waiting for transfers between devices, shards(): lax.psum_scatter(grad_query, ('dp', 'tensor'), scatter_dimension=0, tiled...  142 us
    reduce_scatter x1, waiting for transfers between devices, shards(): lax.psum_scatter(grad_output, ('dp', 'tensor'), scatter_dimension=0, tile...  141 us
    reduce_scatter x1, waiting for transfers between devices, shards(): lax.psum_scatter(grad_key, ('dp', 'tensor'), scatter_dimension=0, tiled=T...  113 us
    reduce_scatter x1, waiting for transfers between devices, shards(): lax.psum_scatter(grad_value, ('dp', 'tensor'), scatter_dimension=0, tiled...  112 us
    unnamed x2, blocking collectives  82.4 us
    reduce_scatter x1, waiting for transfers between devices, shards(): lax.psum_scatter(grad_down, 'dp', scatter_dimension=1, tiled=True)  65.7 us
    reduce_scatter x1, waiting for transfers between devices, shards(): lax.psum_scatter(grad_up, 'dp', scatter_dimension=0, tiled=True)  60.7 us
    all_gather x1, waiting for transfers between devices, shards(): lax.all_gather(w_query, ('dp', 'tensor'), axis=0, tiled=True)  38.5 us
  transfers between devices with their start and end apart: 17, of which 16 were waited for; matrix products, arithmetic and copies ran while one was open for 12% of the time, Pallas kernels for 0%

commit v1 on v0

--- a/solution.py
+++ b/solution.py
@@ -152,7 +152,34 @@
     ).astype(jnp.float32)
     layer_out = (resid_sum + mlp_sum).astype(jnp.bfloat16)
     grad_float = cotangent.astype(jnp.float32)
-    grad_all = lax.all_gather(cotangent, "tensor", axis=0, tiled=True)
+    d_next, spare, z_new = (
+        jax.lax.axis_size("tensor"),
+        jax.lax.axis_index("tensor"),
+        cotangent.shape[0],
+    )
+    row_list = []
+    for i0, to_i in enumerate(cotangent.shape):
+        row_list.append(to_i * d_next if i0 == 0 else to_i)
+    grad_all = lax.dynamic_update_slice_in_dim(
+        jnp.zeros(row_list, cotangent.dtype), cotangent, spare * z_new, axis=0
+    )
+    carry_in = frame_out = cotangent
+    for c in range(1, d_next // 2 + 1):
+        sides = []
+        for i0 in range(d_next):
+            sides.append((i0, (i0 + 1) % d_next))
+        carry_in = jax.lax.ppermute(carry_in, "tensor", sides)
+        grad_all = lax.dynamic_update_slice_in_dim(
+            grad_all, carry_in, (spare - c) % d_next * z_new, axis=0
+        )
+        if 2 * c < d_next:
+            table = []
+            for i0 in range(d_next):
+                table.append((i0, (i0 - 1) % d_next))
+            frame_out = jax.lax.ppermute(frame_out, "tensor", table)
+            grad_all = lax.dynamic_update_slice_in_dim(
+                grad_all, frame_out, (spare + c) % d_next * z_new, axis=0
+            )
     grad_down = jnp.einsum("sf,sd->fd", act_low, grad_all, preferred_element_type=jnp.float32)
     g_act = jnp.einsum("sd,fd->sf", grad_all, w_down, preferred_element_type=jnp.float32)
     g_gate = (g_act * up_val * sig_gate * (1.0 + gate_val * (1.0 - sig_gate))).astype(jnp.bfloat16)

time: 1260 us -> 1240 us (0.984)
  waiting for transfers between devices: 878 us -> 856 us
    ppermute x0 -> x3, waiting for transfers between devices: none -> 37.9 us  [the longest x1 20.6 us: shards(): frame_out = jax.lax.ppermute(frame_out, 'tensor', table)]
    all_gather x1, waiting for transfers between devices: 34.7 us -> 3.98 us  [shards(): rows_all = lax.all_gather(normed_two, 'tensor', axis=0, tiled=True)]
    all_gather x1 -> x0, waiting for transfers between devices: 28.6 us -> none  [shards(): grad_all = lax.all_gather(cotangent, 'tensor', axis=0, tiled=True)]
  transfers between devices with their start and end apart: 17 -> 19, of which waited for: 16 -> 18; matrix products, arithmetic and copies ran while one was open for 12% -> 12% of each run, Pallas kernels for 0% -> 0%
where the time goes in v1:
time: 1240 us
  waiting for transfers between devices  856 us (69%)
  matrix products  160 us (13%)
  blocking collectives  123 us (10%)
  local copies, waits for them, and re-layouts  58.1 us (5%)
  other arithmetic  21.6 us (2%)
  between operations  14.4 us (1%)
    reduce_scatter x1, waiting for transfers between devices, shards(): lax.psum_scatter(grad_query, ('dp', 'tensor'), scatter_dimension=0, tiled...  142 us
    reduce_scatter x1, waiting for transfers between devices, shards(): lax.psum_scatter(grad_output, ('dp', 'tensor'), scatter_dimension=0, tile...  141 us
    reduce_scatter x1, waiting for transfers between devices, shards(): lax.psum_scatter(grad_key, ('dp', 'tensor'), scatter_dimension=0, tiled=T...  114 us
    reduce_scatter x1, waiting for transfers between devices, shards(): lax.psum_scatter(grad_value, ('dp', 'tensor'), scatter_dimension=0, tiled...  112 us
    unnamed x2, blocking collectives  82.4 us
    reduce_scatter x1, waiting for transfers between devices, shards(): lax.psum_scatter(grad_down, 'dp', scatter_dimension=1, tiled=True)  65.6 us
    reduce_scatter x1, waiting for transfers between devices, shards(): lax.psum_scatter(grad_up, 'dp', scatter_dimension=0, tiled=True)  60.7 us
    all_gather x1, waiting for transfers between devices, shards(): lax.all_gather(w_query, ('dp', 'tensor'), axis=0, tiled=True)  38.5 us
  transfers between devices with their start and end apart: 19, of which 18 were waited for; matrix products, arithmetic and copies ran while one was open for 12% of the time, Pallas kernels for 0%

profile of v1, /device:TPU:0, one launch (start us, length us, event | category | flops | bytes accessed | tf_op | source)
XLA Modules:
  0.0 1240.9 jit_solution(2068072983018890646)
XLA Ops:
  12.6 42.1 %all-reduce.5 = (bf16[1536]{0:T(1024)(128)(2,1)S(1)}, bf16[1536]{0:T(1024)(128)(2,1)S(1)}) all-reduce(bf16[1536]{0:T(1024)(128)(2,1)S(1)} %dynamic-update-slice, bf16[1536]{0:T(1024)(128)(2,1)S(1)} %dynamic-update-slice.1), channel_id=1, replica_groups=mesh['dp'=8,'tensor'=4] {'dp','tensor'}, use_global_device_ids=true, to_apply=%add | all-reduce | flops 3072 | bytes 12288
  58.7 11.9 all-gather.8.cloned.1.call-done
  73.7 19.5 %all_gather.30 = bf16[512,768]{0,1:T(8,128)(2,1)} all-gather(bf16[128,768]{0,1:T(8,128)(2,1)S(1)} %bitcast.215), channel_id=1, replica_groups=mesh['dp'=8,'tensor'=4] {'tensor'}, dimensions={0}, use_global_device_ids=true | all-gather | bytes 983040 | tf_op jit(solution)/shard_map/all_gather | solution.py:88
  95.4 35.9 %all-gather.10.cloned.1.call-done = bf16[1536,768]{1,0:T(8,128)(2,1)} async-done(((bf16[48,768]{1,0:T(8,128)(2,1)}), bf16[1536,768]{1,0:T(8,128)(2,1)}) %all-gather.10.cloned.1.call-update) | async-done | bytes 2359312 | tf_op jit(solution)/shard_map/all_gather | solution.py:62
  133.5 21.3 %all_gather.32 = bf16[512,768]{1,0:T(8,128)(2,1)} all-gather(bf16[128,768]{1,0:T(8,128)(2,1)S(1)} %convolution_convert_fusion.2), channel_id=1, replica_groups=mesh['dp'=8,'tensor'=4] {'tensor'}, dimensions={0}, use_global_device_ids=true | all-gather | bytes 983040 | tf_op jit(solution)/shard_map/all_gather | solution.py:89
  159.3 38.5 %all-gather.6.cloned.1.call-done = bf16[1536,1536]{1,0:T(8,128)(2,1)} async-done(((bf16[48,1536]{1,0:T(8,128)(2,1)}), bf16[1536,1536]{1,0:T(8,128)(2,1)}) %all-gather.6.cloned.1.call-update) | async-done | bytes 4718608 | tf_op jit(solution)/shard_map/all_gather | solution.py:60
  205.0 48.8 %while.30 = (s32[]{:T(128)}, bf16[8,256,96]{1,2,0:T(8,128)(2,1)}, f32[8,256]{1,0:T(8,128)}, bf16[8,256,96]{2,1,0:T(8,128)(2,1)}, bf16[8,512,96]{2,1,0:T(8,128)(2...) while((s32[]{:T(128)}, bf16[8,256,96]{1,2,0:T(8,128)(2,1)}, ...), condition=%wide.region_4.5_spmd.clone.clone, body=%wide.region_1.4_spmd.clone.sunk.clone | while | flops 51379968 | bytes 2338905 | solution.py:136
  274.7 10.7 collective-permute-done
  289.4 20.6 %collective-permute-done.1 = bf16[128,1536]{1,0:T(8,128)(2,1)} collective-permute-done((bf16[128,1536]{1,0:T(8,128)(2,1)}, bf16[128,1536]{1,0:T(8,128)(2,1)}, u32[]{:S(2)}, u32[]{:S(2)}) %collective-permute-start.1) | collective-permute-done | bytes 393248 | tf_op jit(solution)/shard_map/ppermute | solution.py:179
  311.7 6.6 collective-permute-done.2
  343.6 29.1 %reduce-scatter.18.cloned.1.call-done = bf16[128,1536]{1,0:T(8,128)(2,1)} async-done(((bf16[512,1536]{1,0:T(8,128)(2,1)}), bf16[128,1536]{1,0:T(8,128)(2,1)}) %reduce-scatter.18.cloned.1.call-update) | async-done | bytes 393232 | tf_op jit(solution)/shard_map/reduce_scatter | solution.py:189
  374.8 34.5 %reduce-scatter.16.cloned.1.call-done = bf16[128,1536]{1,0:T(8,128)(2,1)} async-done(((bf16[512,1536]{1,0:T(8,128)(2,1)}), bf16[128,1536]{1,0:T(8,128)(2,1)}) %reduce-scatter.16.cloned.1.call-update) | async-done | bytes 393232 | tf_op jit(solution)/shard_map/reduce_scatter | solution.py:147
  416.3 61.5 %while.31 = (s32[]{:T(128)}, f32[8,256,96]{1,2,0:T(8,128)}, bf16[8,512,96]{1,2,0:T(8,128)(2,1)}, bf16[8,512,96]{1,2,0:T(8,128)(2,1)}, bf16[8,256,96]{2,1,0:T(8,1...) while((s32[]{:T(128)}, f32[8,256,96]{1,2,0:T(8,128)}, ...), condition=%wide.region_11.12_spmd.clone.clone, body=%wide.region_9.11_spmd.clone.sunk.clone | while | flops 127082240 | bytes 5417073 | solution.py:239
  481.8 5.9 fusion.85
  488.9 5.9 fusion.86
  496.1 6.0 fusion.87
  506.8 20.6 %reduce-scatter.36.cloned.1.call-done = bf16[128,768]{1,0:T(8,128)(2,1)} async-done(((bf16[512,768]{1,0:T(8,128)(2,1)}), bf16[128,768]{1,0:T(8,128)(2,1)}) %reduce-scatter.36.cloned.1.call-update) | async-done | bytes 196624
  553.5 40.2 %all-reduce.4 = (f32[1536]{0:T(1024)}, f32[1536]{0:T(1024)}) all-reduce(f32[1536]{0:T(1024)} %get-tuple-element.201, f32[1536]{0:T(1024)} %get-tuple-element.199), channel_id=6, replica_groups=mesh['dp'=8,'tensor'=4] {'dp','tensor'}, use_global_device_ids=true, to_apply=%region_16.17.clone | all-reduce | flops 3072 | bytes 24576
  598.9 60.7 %reduce-scatter.30.cloned.1.call-done = f32[192,1024]{1,0:T(8,128)} async-done(((f32[1536,1024]{1,0:T(8,128)}), f32[192,1024]{1,0:T(8,128)}) %reduce-scatter.30.cloned.1.call-update) | async-done | bytes 786448 | tf_op jit(solution)/shard_map/reduce_scatter | solution.py:292
  659.5 65.6 %reduce-scatter.32.cloned.1.call-done = f32[1024,192]{0,1:T(8,128)} async-done(((f32[1024,1536]{0,1:T(8,128)}), f32[1024,192]{0,1:T(8,128)}) %reduce-scatter.32.cloned.1.call-update) | async-done | bytes 786448 | tf_op jit(solution)/shard_map/reduce_scatter | solution.py:293
  725.1 113.8 %reduce-scatter.22.cloned.1.call-done = f32[48,768]{1,0:T(8,128)} async-done(((f32[1536,768]{1,0:T(8,128)}), f32[48,768]{1,0:T(8,128)}) %reduce-scatter.22.cloned.1.call-update) | async-done | bytes 147472 | tf_op jit(solution)/shard_map/reduce_scatter | solution.py:284
  838.9 112.3 %reduce-scatter.24.cloned.1.call-done = f32[48,768]{1,0:T(8,128)} async-done(((f32[1536,768]{1,0:T(8,128)}), f32[48,768]{1,0:T(8,128)}) %reduce-scatter.24.cloned.1.call-update) | async-done | bytes 147472 | tf_op jit(solution)/shard_map/reduce_scatter | solution.py:285
  951.2 141.7 %reduce-scatter.20.cloned.1.call-done = f32[48,1536]{1,0:T(8,128)} async-done(((f32[1536,1536]{1,0:T(8,128)}), f32[48,1536]{1,0:T(8,128)}) %reduce-scatter.20.cloned.1.call-update) | async-done | bytes 294928 | tf_op jit(solution)/shard_map/reduce_scatter | solution.py:283
  1092.9 141.5 %reduce-scatter.26.cloned.1.call-done = f32[48,1536]{1,0:T(8,128)} async-done(((f32[1536,1536]{1,0:T(8,128)}), f32[48,1536]{1,0:T(8,128)}) %reduce-scatter.26.cloned.1.call-update) | async-done | bytes 294928 | tf_op jit(solution)/shard_map/reduce_scatter | solution.py:286
  (288 shorter events, 241.4 us)
Async XLA Ops:
  7.2 322.1 %copy-start = (bf16[1024,1536]{1,0:T(8,128)(2,1)S(1)}, bf16[1024,1536]{1,0:T(8,128)(2,1)}, u32[]{:S(2)}) copy-start(bf16[1024,1536]{1,0:T(8,128)(2,1)} %param.26) | copy-start | bytes 9437188
  7.2 63.4 %all-gather.8.cloned.1.call-start = ((), (), s32[]{:S(2)}) async-start(), calls=%async_computation.12 | async-start | bytes 2433024 | tf_op jit(solution)/shard_map/all_gather | solution.py:61
  7.9 123.4 %all-gather.10.cloned.1.call-start = ((), (), s32[]{:S(2)}) async-start(), calls=%async_computation.13 | async-start | bytes 2433024 | tf_op jit(solution)/shard_map/all_gather | solution.py:62
  8.7 189.1 %all-gather.6.cloned.1.call-start = ((), (), s32[]{:S(2)}) async-start(), calls=%async_computation.11 | async-start | bytes 4866048 | tf_op jit(solution)/shard_map/all_gather | solution.py:60
  9.4 253.0 %all-gather.12.cloned.1.call-start = ((), (), s32[]{:S(2)}) async-start(), calls=%async_computation.14 | async-start | bytes 4866048 | tf_op jit(solution)/shard_map/all_gather | solution.py:63
  10.0 313.1 %all-gather.14.cloned.1.call-start = ((), (), s32[]{:S(2)}) async-start(), calls=%async_computation.15 | async-start | bytes 1966080 | tf_op jit(solution)/shard_map/all_gather | solution.py:141
  267.7 104.9 %reduce-scatter.18.cloned.1.call-start = ((), (), s32[]{:S(2)}) async-start(), calls=%async_computation.17 | async-start | bytes 1966080 | tf_op jit(solution)/shard_map/reduce_scatter | solution.py:189
  267.8 17.7 %collective-permute-start = (bf16[128,1536]{1,0:T(8,128)(2,1)}, bf16[128,1536]{1,0:T(8,128)(2,1)}, u32[]{:S(2)}, u32[]{:S(2)}) collective-permute-start(bf16[128,1536]{1,0:T(8,128)(2,1)} %param.27), channel_id=1, source_target_pairs={{0,1},{1,2},{2,3},{3,0},{4,5},{5,6},{6,7},{7,4},{8,9},{9,10},{10,1... | collective-permute-start | bytes 1179656 | tf_op jit(solution)/shard_map/ppermute | solution.py:171
  269.2 40.7 %collective-permute-start.1 = (bf16[128,1536]{1,0:T(8,128)(2,1)}, bf16[128,1536]{1,0:T(8,128)(2,1)}, u32[]{:S(2)}, u32[]{:S(2)}) collective-permute-start(bf16[128,1536]{1,0:T(8,128)(2,1)} %param.27), channel_id=1, source_target_pairs={{0,3},{1,0},{2,1},{3,2},{4,7},{5,4},{6,5},{7,6},{8,11},{9,8},{10,9... | collective-permute-start | bytes 1179656 | tf_op jit(solution)/shard_map/ppermute | solution.py:179
  285.5 32.9 %collective-permute-start.2 = (bf16[128,1536]{1,0:T(8,128)(2,1)}, bf16[128,1536]{1,0:T(8,128)(2,1)S(1)}, u32[]{:S(2)}, u32[]{:S(2)}) collective-permute-start(bf16[128,1536]{1,0:T(8,128)(2,1)} %collective-permute-done), channel_id=1, source_target_pairs={{0,1},{1,2},{2,3},{3,0},{4,5},{5,6},{6,7},{7,4},{8,9},{9,10},{10,1... | collective-permute-start | bytes 1179656 | tf_op jit(solution)/shard_map/ppermute | solution.py:171
  339.2 70.0 %reduce-scatter.16.cloned.1.call-start = ((), (), s32[]{:S(2)}) async-start(), calls=%async_computation.16 | async-start | bytes 1966080 | tf_op jit(solution)/shard_map/reduce_scatter | solution.py:147
  343.4 65.9 %copy-start.23 = (f32[128]{0:T(128)S(1)}, f32[128]{0:T(128)}, u32[]{:S(2)}) copy-start(f32[128]{0:T(128)} %copy-done.22) | copy-start | bytes 1540
  343.5 65.9 %copy-start.24 = (f32[128]{0:T(128)S(1)}, f32[128]{0:T(128)}, u32[]{:S(2)}) copy-start(f32[128]{0:T(128)} %get-tuple-element.263) | copy-start | bytes 1540
  343.5 158.9 %reduce-scatter.34.cloned.1.call-start = ((), (), s32[]{:S(2)}) async-start(), calls=%async_computation.25 | async-start | bytes 983040
  411.5 127.0 %copy-start.5 = (f32[128,1536]{1,0:T(8,128)}, f32[128,1536]{1,0:T(8,128)S(1)}, u32[]{:S(2)}) copy-start(f32[128,1536]{1,0:T(8,128)S(1)} %get-tuple-element.252) | copy-start | bytes 2359300
  480.2 47.2 %reduce-scatter.36.cloned.1.call-start = ((), (), s32[]{:S(2)}) async-start(), calls=%async_computation.26 | async-start | bytes 983040
  481.5 117.4 %reduce-scatter.28.cloned.1.call-start = ((), (), s32[]{:S(2)}) async-start(), calls=%async_computation.22 | async-start | bytes 7077888 | tf_op jit(solution)/shard_map/reduce_scatter | solution.py:291
  487.7 171.8 %reduce-scatter.30.cloned.1.call-start = ((), (), s32[]{:S(2)}) async-start(), calls=%async_computation.23 | async-start | bytes 7077888 | tf_op jit(solution)/shard_map/reduce_scatter | solution.py:292
  494.8 230.2 %reduce-scatter.32.cloned.1.call-start = ((), (), s32[]{:S(2)}) async-start(), calls=%async_computation.24 | async-start | bytes 7077888 | tf_op jit(solution)/shard_map/reduce_scatter | solution.py:293
  502.0 336.8 %reduce-scatter.22.cloned.1.call-start = ((), (), s32[]{:S(2)}) async-start(), calls=%async_computation.19 | async-start | bytes 4866048 | tf_op jit(solution)/shard_map/reduce_scatter | solution.py:284
  506.8 444.4 %reduce-scatter.24.cloned.1.call-start = ((), (), s32[]{:S(2)}) async-start(), calls=%async_computation.20 | async-start | bytes 4866048 | tf_op jit(solution)/shard_map/reduce_scatter | solution.py:285
  531.4 561.5 %reduce-scatter.20.cloned.1.call-start = ((), (), s32[]{:S(2)}) async-start(), calls=%async_computation.18 | async-start | bytes 9732096 | tf_op jit(solution)/shard_map/reduce_scatter | solution.py:283
  538.2 696.2 %reduce-scatter.26.cloned.1.call-start = ((), (), s32[]{:S(2)}) async-start(), calls=%async_computation.21 | async-start | bytes 9732096 | tf_op jit(solution)/shard_map/reduce_scatter | solution.py:286
  551.1 683.3 %copy-start.1 = (bf16[1024,1536]{1,0:T(8,128)(2,1)S(1)}, bf16[1024,1536]{1,0:T(8,128)(2,1)}, u32[]{:S(2)}) copy-start(bf16[1024,1536]{1,0:T(8,128)(2,1)} %param.26) | copy-start | bytes 9437188
  (28 other events, 265.3 us)
Sparse Core Ops, SparseCore 0:
  10.8 59.7 all-gather.7
  73.4 57.8 all-gather.9
  134.1 63.6 all-gather.5
  200.4 61.8 all-gather.11
  267.8 55.2 all-gather.13
  339.4 33.2 reduce-scatter.17
  375.0 34.2 reduce-scatter.15
  480.4 21.9 reduce-scatter.33
  504.7 22.6 reduce-scatter.35
  531.2 62.1 reduce-scatter.27
  597.4 62.0 reduce-scatter.29
  663.3 61.7 reduce-scatter.31
  731.1 107.6 reduce-scatter.21
  844.8 106.3 reduce-scatter.23
  957.5 135.3 reduce-scatter.19
  1099.2 135.0 reduce-scatter.25
